TPU v7x, 128 devices: a whole 4x4x4 slice. The times are simulated.
128 devices in a mesh: dp: 16 (over z_hi, x, core), group: 8 (over y, z_lo).
Axes of the slice: x: 4, y: 4, z: 4 (z_hi: 2, z_lo: 2; z = z_hi * 2 + z_lo), core: 2. Of those that a mesh axis runs over, the one named last changes fastest.
Arguments:
- volume: bfloat16 [256, 256, 2, 256], P('group'), may hold values from -6 to 6
- images: bfloat16 [2048, 256, 256], P(('dp', 'group')), may hold values from -6 to 6
- orientation: int32 [32], replicated, may hold values from 0 to 359
- batch_slot: int32 [2048], P(('dp', 'group')), may hold values from 0 to 1
- ctf_class: int32 [2048], P(('dp', 'group')), may hold values from 0 to 15
Outputs:
- grad_volume: float32 [256, 256, 2, 256], P('group', 'dp')
All inputs are finite; a program needn't handle non-finite values.
Results may differ from a plain program's by a relative error of at most 0.0095.
Values may be sent and summed in bfloat16 or wider, within the bound.
A program may use at most 128 MiB of HBM per device.

v0:
```python
import math

import jax
import jax.numpy as jnp
from jax import lax
from jax.sharding import PartitionSpec as P

NROT = 360
ORI_DEV = 2


PRIOR_WEIGHT = 0.25


def axis_weights(base, frac, start, span):
    cells = jnp.arange(span, dtype=jnp.int32) + start
    lower = (cells[None, :, None] == base[:, None, :]).astype(jnp.float32) * (1.0 - frac)[
        :, None, :
    ]
    upper = (cells[None, :, None] == (base + 1)[:, None, :]).astype(jnp.float32) * frac[:, None, :]
    return lower + upper


def slice_matrix(orient_ids, length, z_start, z_len, y_start, y_len):
    tilt_angle = jnp.pi * (orient_ids.astype(jnp.float32) + 0.5) / NROT
    offset = (jnp.arange(length, dtype=jnp.int32) - length // 2).astype(jnp.float32)
    coord_z = length / 2 + offset[None, :] * jnp.sin(tilt_angle)[:, None]
    coord_y = length / 2 + offset[None, :] * jnp.cos(tilt_angle)[:, None]
    floor_z = jnp.floor(coord_z)
    floor_y = jnp.floor(coord_y)
    weight_z = axis_weights(floor_z.astype(jnp.int32), coord_z - floor_z, z_start, z_len)
    weight_y = axis_weights(floor_y.astype(jnp.int32), coord_y - floor_y, y_start, y_len)
    full = weight_z[:, :, None, :] * weight_y[:, None, :, :]
    full = full.reshape(orient_ids.shape[0], z_len * y_len, length)
    high = full.astype(jnp.bfloat16)
    low = (full - high.astype(jnp.float32)).astype(jnp.bfloat16)
    return (high, low)


def extract(planes, orient_ids, z_start, z_len, length):
    high, low = slice_matrix(orient_ids, length, z_start, z_len, 0, length)
    result = jnp.einsum("krj,rm->kjm", high, planes, preferred_element_type=jnp.float32)
    result = result + jnp.einsum("krj,rm->kjm", low, planes, preferred_element_type=jnp.float32)
    return result.reshape(orient_ids.shape[0], length, 2, length)


def backproject(slice_grads, orient_ids, z_start, z_len, y_start, y_len):
    length = slice_grads.shape[-1]
    count = slice_grads.shape[0]
    high, low = slice_matrix(orient_ids, length, z_start, z_len, y_start, y_len)
    flat = slice_grads.reshape(count, length, 2 * length)
    added = jnp.einsum("krj,kjm->rm", high, flat, preferred_element_type=jnp.float32)
    added = added + jnp.einsum("krj,kjm->rm", low, flat, preferred_element_type=jnp.float32)
    return added.reshape(z_len * y_len, 2, length)


def contrast(classes, length):
    offset = (jnp.arange(length, dtype=jnp.int32) - length // 2).astype(jnp.float32)
    radius = (offset[:, None] ** 2 + offset[None, :] ** 2) / (length * length)
    defocus = 30.0 + 10.0 * classes.astype(jnp.float32)
    return -jnp.sin(defocus[:, None, None] * radius[None] + 0.1)


def spectra(images):
    count = images.shape[0]
    length = images.shape[-1]
    freq_idx = jnp.arange(length, dtype=jnp.int32) - length // 2
    sample = jnp.arange(length, dtype=jnp.int32)
    phase_idx = freq_idx[:, None] * sample[None, :] % length
    dft_angle = -2.0 * jnp.pi / length * phase_idx.astype(jnp.float32)
    norm_factor = 1.0 / math.sqrt(length)
    basis_re = jnp.cos(dft_angle) * norm_factor
    basis_im = jnp.sin(dft_angle) * norm_factor
    stacked = jnp.stack([basis_re, basis_im], axis=0)
    stacked_hi = stacked.astype(jnp.bfloat16)
    stacked_lo = (stacked - stacked_hi.astype(jnp.float32)).astype(jnp.bfloat16)
    half = jnp.einsum("cjm,pmn->pjcn", stacked_hi, images, preferred_element_type=jnp.float32)
    half = half + jnp.einsum(
        "cjm,pmn->pjcn", stacked_lo, images, preferred_element_type=jnp.float32
    )
    trans_re = basis_re.T
    trans_im = basis_im.T
    complex_mat = jnp.concatenate(
        [
            jnp.concatenate([trans_re, trans_im], axis=1),
            jnp.concatenate([-trans_im, trans_re], axis=1),
        ],
        axis=0,
    )
    flat = half.reshape(count * length, 2 * length)
    result = jnp.dot(
        flat, complex_mat, precision=lax.Precision.HIGH, preferred_element_type=jnp.float32
    )
    return result.reshape(count, length, 2, length)


def per_device(volume, images, orientation, batch_slot, ctf_class):
    length = volume.shape[-1]
    slab_len = volume.shape[0]
    strip_len = length // lax.axis_size("dp")
    slab_start = lax.axis_index("group") * slab_len
    strip_start = lax.axis_index("dp") * strip_len
    own_orient = lax.dynamic_slice_in_dim(orientation, lax.axis_index("dp") * ORI_DEV, ORI_DEV)
    planes = volume.reshape(slab_len * length, 2 * length)
    partial_value = extract(planes, own_orient, slab_start, slab_len, length)
    slices = lax.psum(partial_value, "group")
    spectrum = spectra(images)
    factor = contrast(ctf_class, length)[:, :, None, :]
    predicted = jnp.take(slices, batch_slot, axis=0)
    residual = factor * predicted - spectrum
    weighted = factor * residual
    onehot = (batch_slot[:, None] == jnp.arange(ORI_DEV, dtype=jnp.int32)[None, :]).astype(
        jnp.float32
    )
    local_grads = jnp.einsum("ps,pjcx->sjcx", onehot, weighted, precision=lax.Precision.HIGHEST)
    slice_grads = lax.psum(local_grads, "group").astype(jnp.bfloat16)
    summed = backproject(slice_grads, own_orient, slab_start, slab_len, 0, length)
    summed = summed.reshape(slab_len, length, 2, length)
    strip = lax.psum_scatter(summed, "dp", scatter_dimension=1, tiled=True)
    prior_part = lax.dynamic_slice_in_dim(volume, strip_start, strip_len, 1).astype(jnp.float32)
    return strip + PRIOR_WEIGHT * prior_part


def solution(mesh):
    in_specs = (
        P("group", None, None, None),
        P(("dp", "group"), None, None),
        P(),
        P(("dp", "group")),
        P(("dp", "group")),
    )
    out_specs = P("group", "dp", None, None)
    return jax.shard_map(
        per_device, mesh=mesh, in_specs=in_specs, out_specs=out_specs, check_vma=False
    )
```

profile of v0, /device:TPU:1, one launch (start us, length us, event | category | flops | bytes accessed | tf_op | source)
XLA Modules:
  0.0 441.9 jit_solution(7657171384069393221)
XLA Ops:
  6.5 0.9 fusion.33
  7.6 14.1 %reshape.407 = bf16[8192,512,1]{1,0,2:T(8,128)(2,1)} reshape(bf16[32,256,2,256]{3,2,1,0:T(2,128)(2,1)} %param.5) | data formatting | bytes 16777216 | tf_op jit(solution)/shard_map/reshape | solution.py:104
  21.7 0.1 select_add_fusion
  21.9 8.3 %subtract_convert_fusion = (bf16[2,32,256,256]{3,2,1,0:T(8,128)(2,1)S(1)}, bf16[2,32,256,256]{3,2,1,0:T(8,128)(2,1)S(1)}, f32[2,32,256,256]{3,2,1,0:T(8,128)}) fusion(f32[2,256,256]{2,1,0:T(8,128)S(1)} %select_add_fusion, f32[2,32,256]{2,1,0:T(8,128)S(1)} %select_add_fusion.1), kind=kLoop, calls=%fused_computation.5 | loop fusion | flops 20971520 | bytes 34144256 | tf_op jit(solution)/shard_map/convert_element_type | solution.py:36
  30.1 4.5 %fusion.34 = f32[2,256,512]{2,1,0:T(8,128)S(1)} fusion(bf16[2,8192,256]{2,1,0:T(8,128)(2,1)S(1)} %bitcast.66, bf16[8192,512,1]{1,0,2:T(8,128)(2,1)S(1)} %bitcast.63), kind=kOutput, calls=%fused_computation.81 | convolution fusion | flops 4294967296 | bytes 17825792 | tf_op jit(solution)/shard_map/krj,rm->kjm/dot_general | solution.py:42
  34.7 4.5 %convolution_add_fusion = f32[2,256,512]{2,1,0:T(8,128)S(1)} fusion(f32[2,256,512]{2,1,0:T(8,128)S(1)} %fusion.34, bf16[2,8192,256]{2,1,0:T(8,128)(2,1)S(1)} %bitcast.64, bf16[8192,512,1]{1,0,2:T(8,128)(2,1)S(1)} %bitcast.63), kind=kOutput, calls=%fused_computation.16 | convolution fusion | flops 4295229440 | bytes 18874368 | tf_op jit(solution)/shard_map/krj,rm->kjm/dot_general | solution.py:43
  39.2 1.1 copy.54
  40.3 0.5 reduce-scatter.2.cloned.1.call-start
  40.8 1.1 cosine_multiply_fusion.1
  41.9 1.1 sine_multiply_fusion
  43.1 5.4 %fusion.4 = f32[2,256,16,256]{1,3,2,0:T(8,128)} fusion(bf16[16,256,256]{2,1,0:T(8,128)(2,1)S(1)} %copy-done, f32[1,256,256]{2,1,0:T(8,128)S(1)} %get-tuple-element.20, f32[1,256,256]{2,1,0:T(8,128)S(1)} %get-tuple-element.19), kind=kOutput, calls=%fused_computation.14 | convolution fusion | flops 1074266112 | bytes 11010048 | tf_op jit(solution)/shard_map/cjm,pmn->pjcn/dot_general | solution.py:77
  48.6 4.8 %add_bitcast_fusion = f32[16,256,2,256]{1,3,0,2:T(8,128)S(1)} fusion(f32[2,256,16,256]{1,3,2,0:T(8,128)} %fusion.4, bf16[16,256,256]{2,1,0:T(8,128)(2,1)S(1)} %copy-done, f32[1,256,256]{2,1,0:T(8,128)S(1)} %get-tuple-element.20, f32[1,256,256]{2,1,0:T(8,128)S(1)} %get-tuple-element.19), kind=kOutput, calls=%fused_computation.10 | convolution fusion | flops 1076494336 | bytes 19398656 | tf_op jit(solution)/shard_map/cjm,pmn->pjcn/dot_general | solution.py:78
  53.4 1.2 slice-done.3
  54.6 7.2 %fusion = (bf16[2,8192,256]{2,1,0:T(8,128)(2,1)}, bf16[2,8192,256]{2,1,0:T(8,128)(2,1)}) fusion(f32[2,32,256,256]{3,2,1,0:T(8,128)S(1)} %bitcast.61), kind=kLoop, calls=%fused_computation.4 | loop fusion | flops 16777216 | bytes 33554432 | tf_op jit(solution)/shard_map/convert_element_type | solution.py:36
  61.8 0.1 maximum_maximum_fusion
  61.9 4.2 copy.25
  66.1 0.1 add_multiply_fusion
  66.3 15.2 %sine_negate_fusion = f32[16,256,256]{2,1,0:T(8,128)} fusion(f32[256,256]{1,0:T(8,128)S(1)} %add_multiply_fusion, f32[16]{0:T(128)S(1)} %multiply_add_fusion.3), kind=kLoop, calls=%fused_computation.12 | loop fusion | flops 3145728 | bytes 4456512 | tf_op jit(solution)/shard_map/neg | solution.py:61
  81.5 36.1 %all-reduce.3.cloned.1.call-done = f32[2,256,2,256]{3,1,2,0:T(8,128)} async-done(((f32[2,256,2,256]{3,1,2,0:T(8,128)}), f32[2,256,2,256]{3,1,2,0:T(8,128)}) %all-reduce.3.cloned.1.call-update) | async-done | bytes 1048592 | tf_op jit(solution)/shard_map/psum | solution.py:106
  117.6 5.5 %gather_fusion = f32[16,256,2,256]{3,1,2,0:T(8,128)} fusion(f32[2,256,2,256]{3,1,2,0:T(8,128)} %all-reduce.3.cloned.1.call-done, s32[1024]{0:T(1024)S(1)} %pad_clamp_fusion), kind=kCustom, calls=%fused_computation | custom fusion | bytes 16777280 | tf_op jit(solution)/shard_map/jit(_take)/gather | solution.py:109
  123.1 19.7 %subtract_multiply_fusion = f32[16,256,2,256]{3,1,2,0:T(8,128)S(1)} fusion(f32[16,256,2,256]{3,1,2,0:T(8,128)} %gather_fusion, f32[16,256,256]{2,1,0:T(8,128)} %sine_negate_fusion, pred[16]{0:T(512)(128)(4,1)S(1)} %compare_and_fusion, f32[16,256,512,1]{1,2,3,0:T(8,128)} %bitcast.65, f32[2,256,512,1]{2,1,0,3:T(8,128)S(1)} %bitcast.69), kind=kOutput, calls=%fused_computation.9 | convolution fusion | flops 6450839552 | bytes 30408720 | tf_op jit(solution)/shard_map/dot_general | solution.py:91
  142.8 6.4 %fusion.1 = f32[2,256,2,256]{3,0,2,1:T(2,128)S(1)} fusion(f32[16,256,2,256]{3,1,2,0:T(8,128)S(1)} %subtract_multiply_fusion, s32[16]{0:T(128)S(1)} %copy-done.2), kind=kOutput, calls=%fused_computation.7 | convolution fusion | flops 50331680 | bytes 9437248 | tf_op jit(solution)/shard_map/ps,pjcx->sjcx/dot_general | solution.py:115
  149.2 55.9 %all-reduce.4 = bf16[2,256,2,256]{3,0,2,1:T(2,128)(2,1)S(1)} all-reduce(f32[2,256,2,256]{3,0,2,1:T(2,128)S(1)} %fusion.1), channel_id=1, replica_groups=mesh['dp'=16,'group'=8] {'group'}, use_global_device_ids=true, to_apply=%region_1.2 | all-reduce | flops 262144 | bytes 1572864 | tf_op jit(solution)/shard_map/psum | solution.py:116
  205.1 0.5 copy.28
  205.7 11.7 %fusion.35 = f32[8192,512,1]{1,0,2:T(8,128)} fusion(bf16[2,8192,256]{2,1,0:T(8,128)(2,1)} %get-tuple-element.6, bf16[2,256,512]{1,2,0:T(8,128)(2,1)S(1)} %bitcast.67), kind=kOutput, calls=%fused_computation.82 | convolution fusion | flops 4294967296 | bytes 25690112 | tf_op jit(solution)/shard_map/krj,kjm->rm/dot_general | solution.py:52
  217.4 14.1 %bitcast_add_fusion = f32[8192,512]{1,0:T(8,128)} fusion(f32[8192,512,1]{1,0,2:T(8,128)} %fusion.35, bf16[2,8192,256]{2,1,0:T(8,128)(2,1)} %get-tuple-element.5, bf16[2,256,512]{1,2,0:T(8,128)(2,1)S(1)} %bitcast.68), kind=kOutput, calls=%fused_computation.1 | convolution fusion | flops 4299161600 | bytes 42467328 | tf_op jit(solution)/shard_map/krj,kjm->rm/dot_general | solution.py:53
  231.4 19.9 %reshape_reshape.3 = f32[32,256,2,256]{3,2,1,0:T(2,128)} reshape(f32[8192,512]{1,0:T(8,128)} %bitcast_add_fusion) | data formatting | bytes 33554432 | tf_op jit(solution)/shard_map/reshape;reshape | solution.py:118
  251.3 17.7 %copy.31 = f32[32,256,2,256]{3,0,2,1:T(8,128)} copy(f32[32,256,2,256]{3,2,1,0:T(2,128)} %reshape_reshape.3) | data formatting | bytes 33554432 | tf_op jit(solution)/shard_map/reshape;reshape | solution.py:118
  269.0 1.6 constant_dynamic-slice_fusion
  270.7 160.8 %reduce-scatter.2.cloned.1.call-done = f32[32,16,2,256]{3,0,2,1:T(8,128)} async-done(((f32[32,256,2,256]{3,0,2,1:T(8,128)}), f32[32,16,2,256]{3,0,2,1:T(8,128)}) %reduce-scatter.2.cloned.1.call-update) | async-done | bytes 1048592 | tf_op jit(solution)/shard_map/reduce_scatter | solution.py:119
  431.5 1.6 multiply_add_fusion
  433.1 1.8 copy.33
  (35 shorter events, 0.4 us)
Async XLA Ops:
  6.5 36.5 %copy-start = (bf16[16,256,256]{2,1,0:T(8,128)(2,1)S(1)}, bf16[16,256,256]{2,1,0:T(8,128)(2,1)}, u32[]{:S(2)}) copy-start(bf16[16,256,256]{2,1,0:T(8,128)(2,1)} %param.6) | copy-start | bytes 6291460
  6.5 111.0 %all-reduce.3.cloned.1.call-start = ((), (), s32[]{:S(2)}) async-start(), calls=%async_computation.1 | async-start | bytes 2097152 | tf_op jit(solution)/shard_map/psum | solution.py:106
  21.7 8.4 %slice-start.4 = ((s8[8388608]{0:T(1024)(128)(4,1)}), s8[4194304]{0:T(1024)(128)(4,1)S(1)}, s32[]{:S(2)}) async-start(s8[8388608]{0:T(1024)(128)(4,1)} %bitcast.62), calls=%async_computation.7 | async-start | bytes 8388608
  21.9 8.3 %slice-start.5 = ((s8[8388608]{0:T(1024)(128)(4,1)}), s8[4194304]{0:T(1024)(128)(4,1)S(1)}, s32[]{:S(2)}) async-start(s8[8388608]{0:T(1024)(128)(4,1)} %bitcast.62), calls=%async_computation.8 | async-start | bytes 8388608
  34.6 8.4 %copy-start.2 = (s32[16]{0:T(128)S(1)}, s32[16]{0:T(128)}, u32[]{:S(2)}) copy-start(s32[16]{0:T(128)} %param.8) | copy-start | bytes 196
  40.3 391.2 %reduce-scatter.2.cloned.1.call-start = ((), (), s32[]{:S(2)}) async-start(), calls=%async_computation.2 | async-start | bytes 17825792 | tf_op jit(solution)/shard_map/reduce_scatter | solution.py:119
  43.1 10.3 %slice-start = ((s8[16777216]{0:T(1024)(128)(4,1)}), s8[4194304]{0:T(1024)(128)(4,1)S(1)}, s32[]{:S(2)}) async-start(s8[16777216]{0:T(1024)(128)(4,1)} %bitcast.60), calls=%async_computation.3 | async-start | bytes 8388608
  43.1 10.3 %slice-start.1 = ((s8[16777216]{0:T(1024)(128)(4,1)}), s8[4194304]{0:T(1024)(128)(4,1)S(1)}, s32[]{:S(2)}) async-start(s8[16777216]{0:T(1024)(128)(4,1)} %bitcast.60), calls=%async_computation.4 | async-start | bytes 8388608
  48.6 4.9 %slice-start.2 = ((s8[16777216]{0:T(1024)(128)(4,1)}), s8[4194304]{0:T(1024)(128)(4,1)S(1)}, s32[]{:S(2)}) async-start(s8[16777216]{0:T(1024)(128)(4,1)} %bitcast.60), calls=%async_computation.5 | async-start | bytes 8388608
  48.6 6.1 %slice-start.3 = ((s8[16777216]{0:T(1024)(128)(4,1)}), s8[4194304]{0:T(1024)(128)(4,1)S(1)}, s32[]{:S(2)}) async-start(s8[16777216]{0:T(1024)(128)(4,1)} %bitcast.60), calls=%async_computation.6 | async-start | bytes 8388608
  61.9 4.2 copy-start.3
  269.0 165.8 %copy-start.1 = (bf16[16,256,256]{2,1,0:T(8,128)(2,1)S(1)}, bf16[16,256,256]{2,1,0:T(8,128)(2,1)}, u32[]{:S(2)}) copy-start(bf16[16,256,256]{2,1,0:T(8,128)(2,1)} %param.6) | copy-start | bytes 6291460
Sparse Core Ops, SparseCore 0:
  40.4 77.1 all-reduce.2
  269.2 162.2 reduce-scatter.1
where the time goes:
time: 448 us; the launch traced here: 442 us
  waiting for transfers between devices  197 us (44%)
  matrix products  71.2 us (16%)
  local copies, waits for them, and re-layouts  67.6 us (15%)
  blocking collectives  55.9 us (12%)
  other arithmetic  36 us (8%)
  between operations  13.9 us (3%)
    reduce_scatter x1, waiting for transfers between devices, per_device(): strip = lax.psum_scatter(summed, 'dp', scatter_dimension=1, tiled=True)  161 us
    psum x1, blocking collectives, per_device(): slice_grads = lax.psum(local_grads, 'group').astype(jnp.bfloat16)  55.9 us
    another operation x2, local copies, waits for them, and re-layouts, per_device(): summed = summed.reshape(slab_len, length, 2, length)  37.6 us
    psum x1, waiting for transfers between devices, per_device(): slices = lax.psum(partial_value, 'group')  36.1 us
    dot_general x1, matrix products, spectra(): jnp.dot(flat, complex_mat, precision=lax.Precision.HIGH, preferred_elemen...  19.7 us
    convert_element_type x2, other arithmetic, slice_matrix(): low = (full - high.astype(jnp.float32)).astype(jnp.bfloat16)  15.4 us
    neg x1, other arithmetic, contrast(): return -jnp.sin(defocus[:, None, None] * radius[None] + 0.1)  15.2 us
    reshape x1, local copies, waits for them, and re-layouts, per_device(): planes = volume.reshape(slab_len * length, 2 * length)  14.1 us
  transfers between devices with their start and end apart: 2, of which 2 were waited for; matrix products, arithmetic and copies ran while one was open for 9% of the time, Pallas kernels for 0%

commit v1 on v0

--- a/solution.py
+++ b/solution.py
@@ -114,9 +114,9 @@
     )
     local_grads = jnp.einsum("ps,pjcx->sjcx", onehot, weighted, precision=lax.Precision.HIGHEST)
     slice_grads = lax.psum(local_grads, "group").astype(jnp.bfloat16)
-    summed = backproject(slice_grads, own_orient, slab_start, slab_len, 0, length)
-    summed = summed.reshape(slab_len, length, 2, length)
-    strip = lax.psum_scatter(summed, "dp", scatter_dimension=1, tiled=True)
+    all_grads = lax.all_gather(slice_grads, "dp", axis=0, tiled=True)
+    strip = backproject(all_grads, orientation, slab_start, slab_len, strip_start, strip_len)
+    strip = strip.reshape(slab_len, strip_len, 2, length)
     prior_part = lax.dynamic_slice_in_dim(volume, strip_start, strip_len, 1).astype(jnp.float32)
     return strip + PRIOR_WEIGHT * prior_part
 

time: 448 us -> 371 us (0.83)
  waiting for transfers between devices: 197 us -> 122 us
  other arithmetic: 36 us -> 50 us
  matrix products: 71.2 us -> 61.3 us
    reduce_scatter x1 -> x0, waiting for transfers between devices: 161 us -> none  [per_device(): strip = lax.psum_scatter(summed, 'dp', scatter_dimension=1, tiled=True)]
    all_gather x0 -> x1, waiting for transfers between devices: none -> 69.1 us  [per_device(): all_grads = lax.all_gather(slice_grads, 'dp', axis=0, tiled=True)]
    another operation x2 -> x1, local copies, waits for them, and re-layouts: 37.6 us -> 1.88 us  [per_device(): strip = strip.reshape(slab_len, strip_len, 2, length)]
    convert_element_type x0 -> x2, local copies, waits for them, and re-layouts: none -> 27 us  [the longest x1 13.5 us: slice_matrix(): low = (full - high.astype(jnp.float32)).astype(jnp.bfloat16)]
    psum x1, waiting for transfers between devices: 36.1 us -> 52.5 us  [per_device(): slices = lax.psum(partial_value, 'group')]
    all_gather x0 -> x1, local copies, waits for them, and re-layouts: none -> 12 us  [per_device(): all_grads = lax.all_gather(slice_grads, 'dp', axis=0, tiled=True)]
    mul x0 -> x1, other arithmetic: none -> 8.22 us  [slice_matrix(): full = weight_z[:, :, None, :] * weight_y[:, None, :, :]]
    dot_general x1, matrix products: 4.5 us -> 9.58 us  [extract(): jnp.einsum('krj,rm->kjm', high, planes, preferred_element_type=jnp.float32)]
  transfers between devices with their start and end apart: 2 -> 2, of which waited for: 2 -> 2; matrix products, arithmetic and copies ran while one was open for 9% -> 12% of each run, Pallas kernels for 0% -> 0%
where the time goes in v1:
time: 371 us; the launch traced here: 369 us
  waiting for transfers between devices  122 us (33%)
  local copies, waits for them, and re-layouts  67.2 us (18%)
  matrix products  61.3 us (17%)
  blocking collectives  55.2 us (15%)
  other arithmetic  50 us (13%)
  between operations  13.6 us (4%)
    all_gather x1, waiting for transfers between devices, per_device(): all_grads = lax.all_gather(slice_grads, 'dp', axis=0, tiled=True)  69.1 us
    psum x1, blocking collectives, per_device(): slice_grads = lax.psum(local_grads, 'group').astype(jnp.bfloat16)  55.2 us
    psum x1, waiting for transfers between devices, per_device(): slices = lax.psum(partial_value, 'group')  52.5 us
    dot_general x1, matrix products, spectra(): jnp.dot(flat, complex_mat, precision=lax.Precision.HIGH, preferred_elemen...  19.7 us
    convert_element_type x2, other arithmetic, slice_matrix(): low = (full - high.astype(jnp.float32)).astype(jnp.bfloat16)  18.6 us
    neg x1, other arithmetic, contrast(): return -jnp.sin(defocus[:, None, None] * radius[None] + 0.1)  15.4 us
    reshape x1, local copies, waits for them, and re-layouts, per_device(): planes = volume.reshape(slab_len * length, 2 * length)  14.1 us
    convert_element_type x1, local copies, waits for them, and re-layouts, slice_matrix(): low = (full - high.astype(jnp.float32)).astype(jnp.bfloat16)  13.5 us
  transfers between devices with their start and end apart: 2, of which 2 were waited for; matrix products, arithmetic and copies ran while one was open for 12% of the time, Pallas kernels for 0%

profile of v1, /device:TPU:1, one launch (start us, length us, event | category | flops | bytes accessed | tf_op | source)
XLA Modules:
  0.0 369.2 jit_solution(14421434989639860121)
XLA Ops:
  6.5 0.9 fusion.37
  7.6 0.3 select_add_fusion.1
  8.0 0.3 select_add_fusion.3
  8.3 6.7 %fusion = (bf16[2,32,256,256]{2,1,3,0:T(8,128)(2,1)}, bf16[2,32,256,256]{2,1,3,0:T(8,128)(2,1)}) fusion(f32[2,256,256]{1,2,0:T(8,128)S(1)} %select_add_fusion.1, f32[2,32,256]{1,2,0:T(8,128)S(1)} %select_add_fusion.3), kind=kLoop, calls=%fused_computation.3 | loop fusion | flops 20971520 | bytes 17367040 | tf_op jit(solution)/shard_map/convert_element_type | solution.py:36
  15.0 13.5 %convert_element_type.183 = bf16[2,8192,256]{1,2,0:T(8,128)(2,1)} reshape(bf16[2,32,256,256]{2,1,3,0:T(8,128)(2,1)} %get-tuple-element.8) | data formatting | bytes 16777216 | tf_op jit(solution)/shard_map/convert_element_type | solution.py:35
  28.5 14.1 %reshape.601 = bf16[8192,512,1]{1,0,2:T(8,128)(2,1)} reshape(bf16[32,256,2,256]{3,2,1,0:T(2,128)(2,1)} %param.5) | data formatting | bytes 16777216 | tf_op jit(solution)/shard_map/reshape | solution.py:104
  42.6 13.5 %convert_element_type.186 = bf16[2,8192,256]{1,2,0:T(8,128)(2,1)} reshape(bf16[2,32,256,256]{2,1,3,0:T(8,128)(2,1)} %get-tuple-element.7) | data formatting | bytes 16777216 | tf_op jit(solution)/shard_map/convert_element_type | solution.py:36
  56.1 9.6 %fusion.38 = f32[2,256,512]{2,1,0:T(8,128)S(1)} fusion(bf16[2,8192,256]{1,2,0:T(8,128)(2,1)} %convert_element_type.183, bf16[8192,512,1]{1,0,2:T(8,128)(2,1)} %reshape.601), kind=kOutput, calls=%fused_computation.99 | convolution fusion | flops 4294967296 | bytes 17825792 | tf_op jit(solution)/shard_map/krj,rm->kjm/dot_general | solution.py:42
  65.7 1.0 copy-done.4
  66.8 4.5 %convolution_add_fusion = f32[2,256,512]{2,1,0:T(8,128)S(1)} fusion(f32[2,256,512]{2,1,0:T(8,128)S(1)} %fusion.38, bf16[2,8192,256]{1,2,0:T(8,128)(2,1)S(1)} %copy-done.4, bf16[8192,512,1]{1,0,2:T(8,128)(2,1)S(1)} %copy-done.2), kind=kOutput, calls=%fused_computation.19 | convolution fusion | flops 4295229440 | bytes 18874368 | tf_op jit(solution)/shard_map/krj,rm->kjm/dot_general | solution.py:43
  71.2 1.1 copy.42
  72.6 1.1 cosine_multiply_fusion.1
  73.7 1.1 sine_multiply_fusion
  74.9 1.3 fusion.5
  76.2 1.5 add_bitcast_fusion
  77.8 3.8 %copy.19 = f32[16,256,2,256]{1,3,2,0:T(8,128)} copy(f32[16,256,2,256]{1,3,0,2:T(8,128)S(1)} %add_bitcast_fusion) | data formatting | bytes 16777216 | tf_op jit(solution)/shard_map/add | solution.py:78
  81.7 15.4 %sine_negate_fusion = f32[16,256,256]{2,1,0:T(8,128)} fusion(f32[256,256]{1,0:T(8,128)S(1)} %add_multiply_fusion, f32[16]{0:T(128)S(1)} %multiply_add_fusion.5), kind=kLoop, calls=%fused_computation.12 | loop fusion | flops 3145728 | bytes 4456512 | tf_op jit(solution)/shard_map/neg | solution.py:61
  97.1 52.5 %all-reduce.3.cloned.1.call-done = f32[2,256,2,256]{3,1,2,0:T(8,128)} async-done(((f32[2,256,2,256]{3,1,2,0:T(8,128)}), f32[2,256,2,256]{3,1,2,0:T(8,128)}) %all-reduce.3.cloned.1.call-update) | async-done | bytes 1048592 | tf_op jit(solution)/shard_map/psum | solution.py:106
  149.7 5.5 %gather_fusion = f32[16,256,2,256]{3,1,2,0:T(8,128)} fusion(f32[2,256,2,256]{3,1,2,0:T(8,128)} %all-reduce.3.cloned.1.call-done, s32[1024]{0:T(1024)S(1)} %pad_clamp_fusion), kind=kCustom, calls=%fused_computation | custom fusion | bytes 16777280 | tf_op jit(solution)/shard_map/jit(_take)/gather | solution.py:109
  155.2 19.7 %subtract_multiply_fusion = f32[16,256,2,256]{3,1,2,0:T(8,128)S(1)} fusion(f32[16,256,2,256]{3,1,2,0:T(8,128)} %gather_fusion, f32[16,256,256]{2,1,0:T(8,128)} %sine_negate_fusion, pred[16]{0:T(512)(128)(4,1)S(1)} %compare_and_fusion, f32[16,256,512,1]{1,2,3,0:T(8,128)} %bitcast.68, f32[2,256,512,1]{2,1,0,3:T(8,128)S(1)} %bitcast.71), kind=kOutput, calls=%fused_computation.9 | convolution fusion | flops 6450839552 | bytes 30408720 | tf_op jit(solution)/shard_map/dot_general | solution.py:91
  174.9 6.5 %fusion.2 = f32[2,256,2,256]{3,0,2,1:T(2,128)S(1)} fusion(f32[16,256,2,256]{3,1,2,0:T(8,128)S(1)} %subtract_multiply_fusion, s32[16]{0:T(128)S(1)} %copy-done.6), kind=kOutput, calls=%fused_computation.7 | convolution fusion | flops 50331680 | bytes 9437248 | tf_op jit(solution)/shard_map/ps,pjcx->sjcx/dot_general | solution.py:115
  181.4 55.2 %all-reduce.4 = bf16[2,256,2,256]{3,0,2,1:T(2,128)(2,1)S(1)} all-reduce(f32[2,256,2,256]{3,0,2,1:T(2,128)S(1)} %fusion.2), channel_id=1, replica_groups=mesh['dp'=16,'group'=8] {'group'}, use_global_device_ids=true, to_apply=%region_1.2 | all-reduce | flops 262144 | bytes 1572864 | tf_op jit(solution)/shard_map/psum | solution.py:116
  236.6 0.9 copy.22
  237.9 0.3 select_add_fusion
  238.2 8.2 %broadcast_multiply_fusion = f32[32,32,16,256]{3,2,1,0:T(8,128)} fusion(f32[32,16,256]{2,1,0:T(8,128)S(1)} %select_add_fusion.2, f32[32,32,256]{2,1,0:T(8,128)S(1)} %select_add_fusion), kind=kLoop, calls=%fused_computation.11 | loop fusion | flops 4194304 | bytes 18350080 | tf_op jit(solution)/shard_map/mul | solution.py:33
  246.5 11.9 %fusion.1 = (bf16[32,512,256]{2,1,0:T(8,128)(2,1)}, bf16[32,512,256]{2,1,0:T(8,128)(2,1)}) fusion(f32[32,32,16,256]{3,2,1,0:T(8,128)} %broadcast_multiply_fusion), kind=kLoop, calls=%fused_computation.6 | loop fusion | flops 16777216 | bytes 33554432 | tf_op jit(solution)/shard_map/convert_element_type | solution.py:36
  258.4 69.1 %all-gather.2.cloned.1.call-done = bf16[32,256,2,256]{3,1,2,0:T(8,128)(2,1)} async-done(((bf16[2,256,2,256]{3,1,2,0:T(8,128)(2,1)}), bf16[32,256,2,256]{3,1,2,0:T(8,128)(2,1)}) %all-gather.2.cloned.1.call-update) | async-done | bytes 8388624 | tf_op jit(solution)/shard_map/all_gather | solution.py:117
  327.4 12.0 %copy.23 = bf16[32,256,2,256]{1,3,2,0:T(8,128)(2,1)} copy(bf16[32,256,2,256]{3,1,2,0:T(8,128)(2,1)} %all-gather.2.cloned.1.call-done) | data formatting | bytes 16777216 | tf_op jit(solution)/shard_map/all_gather | solution.py:117
  339.4 11.4 %convolution_bitcast_fusion = f32[512,512]{1,0:T(8,128)} fusion(bf16[32,512,256]{2,1,0:T(8,128)(2,1)} %get-tuple-element.5, bf16[32,256,512]{1,2,0:T(8,128)(2,1)} %bitcast.69), kind=kOutput, calls=%fused_computation.16 | convolution fusion | flops 4294967296 | bytes 17825792 | tf_op jit(solution)/shard_map/krj,kjm->rm/dot_general | solution.py:53
  350.8 6.9 %fusion.7 = f32[512,512]{1,0:T(8,128)} fusion(f32[512,512]{1,0:T(8,128)} %convolution_bitcast_fusion, bf16[32,512,256]{2,1,0:T(8,128)(2,1)S(1)} %copy-done.5, bf16[32,256,512]{1,2,0:T(8,128)(2,1)S(1)} %bitcast.70), kind=kOutput, calls=%fused_computation.18 | convolution fusion | flops 4295229440 | bytes 18874368 | tf_op jit(solution)/shard_map/krj,kjm->rm/dot_general | solution.py:52
  357.7 1.9 reshape_reshape.3
  359.6 2.8 multiply_add_fusion
  (38 shorter events, 1.1 us)
Async XLA Ops:
  6.5 68.3 %copy-start = (bf16[16,256,256]{2,1,0:T(8,128)(2,1)S(1)}, bf16[16,256,256]{2,1,0:T(8,128)(2,1)}, u32[]{:S(2)}) copy-start(bf16[16,256,256]{2,1,0:T(8,128)(2,1)} %param.6) | copy-start | bytes 6291460
  6.5 143.1 %all-reduce.3.cloned.1.call-start = ((), (), s32[]{:S(2)}) async-start(), calls=%async_computation | async-start | bytes 2097152 | tf_op jit(solution)/shard_map/psum | solution.py:106
  56.1 9.6 %copy-start.2 = (bf16[8192,512,1]{1,0,2:T(8,128)(2,1)S(1)}, bf16[8192,512,1]{1,0,2:T(8,128)(2,1)}, u32[]{:S(2)}) copy-start(bf16[8192,512,1]{1,0,2:T(8,128)(2,1)} %reshape.601) | copy-start | bytes 25165828
  56.1 10.6 %copy-start.4 = (bf16[2,8192,256]{1,2,0:T(8,128)(2,1)S(1)}, bf16[2,8192,256]{1,2,0:T(8,128)(2,1)}, u32[]{:S(2)}) copy-start(bf16[2,8192,256]{1,2,0:T(8,128)(2,1)} %convert_element_type.186) | copy-start | bytes 25165828
  66.8 8.1 %copy-start.6 = (s32[16]{0:T(128)S(1)}, s32[16]{0:T(128)}, u32[]{:S(2)}) copy-start(s32[16]{0:T(128)} %param.8) | copy-start | bytes 196
  72.3 255.1 %all-gather.2.cloned.1.call-start = ((), (), s32[]{:S(2)}) async-start(), calls=%async_computation.1 | async-start | bytes 8912896 | tf_op jit(solution)/shard_map/all_gather | solution.py:117
  77.8 3.8 %copy-start.8 = (s32[16]{0:T(128)S(1)}, s32[16]{0:T(128)}, u32[]{:S(2)}) copy-start(s32[16]{0:T(128)} %param.9) | copy-start | bytes 196
  174.9 62.6 %copy-start.7 = (s32[32]{0:T(128)S(1)}, s32[32]{0:T(128)}, u32[]{:S(2)}) copy-start(s32[32]{0:T(128)} %param.7) | copy-start | bytes 388
  339.4 11.4 %copy-start.3 = (bf16[32,256,2,256]{1,3,2,0:T(8,128)(2,1)S(1)}, bf16[32,256,2,256]{1,3,2,0:T(8,128)(2,1)}, u32[]{:S(2)}) copy-start(bf16[32,256,2,256]{1,3,2,0:T(8,128)(2,1)} %copy.23) | copy-start | bytes 25165828
  339.4 11.4 %copy-start.5 = (bf16[32,512,256]{2,1,0:T(8,128)(2,1)S(1)}, bf16[32,512,256]{2,1,0:T(8,128)(2,1)}, u32[]{:S(2)}) copy-start(bf16[32,512,256]{2,1,0:T(8,128)(2,1)} %get-tuple-element.6) | copy-start | bytes 25165828
  350.8 11.5 %copy-start.1 = (bf16[16,256,256]{2,1,0:T(8,128)(2,1)S(1)}, bf16[16,256,256]{2,1,0:T(8,128)(2,1)}, u32[]{:S(2)}) copy-start(bf16[16,256,256]{2,1,0:T(8,128)(2,1)} %param.6) | copy-start | bytes 6291460
Sparse Core Ops, SparseCore 0:
  72.5 77.1 all-reduce.2
  237.6 89.7 all-gather.1

commit v2 on v1

--- a/solution.py
+++ b/solution.py
@@ -113,8 +113,13 @@
         jnp.float32
     )
     local_grads = jnp.einsum("ps,pjcx->sjcx", onehot, weighted, precision=lax.Precision.HIGHEST)
-    slice_grads = lax.psum(local_grads, "group").astype(jnp.bfloat16)
-    all_grads = lax.all_gather(slice_grads, "dp", axis=0, tiled=True)
+    groups = lax.axis_size("group")
+    dps = lax.axis_size("dp")
+    part = lax.psum_scatter(local_grads, "group", scatter_dimension=1, tiled=True)
+    part = part.astype(jnp.bfloat16)
+    gathered = lax.all_gather(part, ("dp", "group"), axis=0, tiled=False)
+    gathered = gathered.reshape(dps, groups, ORI_DEV, length // groups, 2, length)
+    all_grads = gathered.transpose(0, 2, 1, 3, 4, 5).reshape(dps * ORI_DEV, length, 2, length)
     strip = backproject(all_grads, orientation, slab_start, slab_len, strip_start, strip_len)
     strip = strip.reshape(slab_len, strip_len, 2, length)
     prior_part = lax.dynamic_slice_in_dim(volume, strip_start, strip_len, 1).astype(jnp.float32)

time: 371 us -> 625 us (1.68)
  waiting for transfers between devices: 122 us -> 357 us
  local copies, waits for them, and re-layouts: 67.2 us -> 86.1 us
    all_gather x1, waiting for transfers between devices: 69.1 us -> 306 us  [per_device(): gathered = lax.all_gather(part, ('dp', 'group'), axis=0, tiled=False)]
    unnamed x0 -> x1, blocking collectives: none -> 55.2 us
    psum x1 -> x0, blocking collectives: 55.2 us -> none  [per_device(): slice_grads = lax.psum(local_grads, 'group').astype(jnp.bfloat16)]
    reshape x0 -> x1, local copies, waits for them, and re-layouts: none -> 16.3 us  [per_device(): gathered.reshape(dps, groups, ORI_DEV, length // groups, 2, length)]
    another operation x0 -> x1, local copies, waits for them, and re-layouts: none -> 14.1 us  [backproject(): flat = slice_grads.reshape(count, length, 2 * length)]
    all_gather x1 -> x0, local copies, waits for them, and re-layouts: 12 us -> none  [per_device(): all_grads = lax.all_gather(slice_grads, 'dp', axis=0, tiled=True)]
  transfers between devices with their start and end apart: 2 -> 2, of which waited for: 2 -> 2; matrix products, arithmetic and copies ran while one was open for 12% -> 7% of each run, Pallas kernels for 0% -> 0%
where the time goes in v2:
time: 625 us; the launch traced here: 624 us
  waiting for transfers between devices  357 us (57%)
  local copies, waits for them, and re-layouts  86.1 us (14%)
  matrix products  60.7 us (10%)
  blocking collectives  55.2 us (9%)
  other arithmetic  49.9 us (8%)
  between operations  14.3 us (2%)
    all_gather x1, waiting for transfers between devices, per_device(): gathered = lax.all_gather(part, ('dp', 'group'), axis=0, tiled=False)  306 us
    unnamed x1, blocking collectives  55.2 us
    psum x1, waiting for transfers between devices, per_device(): slices = lax.psum(partial_value, 'group')  51.2 us
    dot_general x1, matrix products, spectra(): jnp.dot(flat, complex_mat, precision=lax.Precision.HIGH, preferred_elemen...  19.7 us
    convert_element_type x2, other arithmetic, slice_matrix(): low = (full - high.astype(jnp.float32)).astype(jnp.bfloat16)  18.6 us
    reshape x1, local copies, waits for them, and re-layouts, per_device(): gathered.reshape(dps, groups, ORI_DEV, length // groups, 2, length)  16.3 us
    neg x1, other arithmetic, contrast(): return -jnp.sin(defocus[:, None, None] * radius[None] + 0.1)  15.4 us
    another operation x1, local copies, waits for them, and re-layouts, backproject(): flat = slice_grads.reshape(count, length, 2 * length)  14.1 us
  transfers between devices with their start and end apart: 2, of which 2 were waited for; matrix products, arithmetic and copies ran while one was open for 7% of the time, Pallas kernels for 0%

profile of v2, /device:TPU:1, one launch (start us, length us, event | category | flops | bytes accessed | tf_op | source)
XLA Modules:
  0.0 623.6 jit_solution(13327542506725151982)
XLA Ops:
  6.5 0.9 fusion.37
  7.6 0.3 select_add_fusion.1
  8.3 6.7 %fusion = (bf16[2,32,256,256]{2,1,3,0:T(8,128)(2,1)}, bf16[2,32,256,256]{2,1,3,0:T(8,128)(2,1)}) fusion(f32[2,256,256]{1,2,0:T(8,128)S(1)} %select_add_fusion.1, f32[2,32,256]{1,2,0:T(8,128)S(1)} %select_add_fusion.3), kind=kLoop, calls=%fused_computation.3 | loop fusion | flops 20971520 | bytes 17367040 | tf_op jit(solution)/shard_map/convert_element_type | solution.py:36
  15.0 13.5 %convert_element_type.183 = bf16[2,8192,256]{1,2,0:T(8,128)(2,1)} reshape(bf16[2,32,256,256]{2,1,3,0:T(8,128)(2,1)} %get-tuple-element.8) | data formatting | bytes 16777216 | tf_op jit(solution)/shard_map/convert_element_type | solution.py:35
  28.5 14.1 %reshape.603 = bf16[8192,512,1]{1,0,2:T(8,128)(2,1)} reshape(bf16[32,256,2,256]{3,2,1,0:T(2,128)(2,1)} %param.5) | data formatting | bytes 16777216 | tf_op jit(solution)/shard_map/reshape | solution.py:104
  42.6 13.5 %convert_element_type.186 = bf16[2,8192,256]{1,2,0:T(8,128)(2,1)} reshape(bf16[2,32,256,256]{2,1,3,0:T(8,128)(2,1)} %get-tuple-element.7) | data formatting | bytes 16777216 | tf_op jit(solution)/shard_map/convert_element_type | solution.py:36
  56.1 9.6 %fusion.38 = f32[2,256,512]{2,1,0:T(8,128)S(1)} fusion(bf16[2,8192,256]{1,2,0:T(8,128)(2,1)} %convert_element_type.183, bf16[8192,512,1]{1,0,2:T(8,128)(2,1)} %reshape.603), kind=kOutput, calls=%fused_computation.101 | convolution fusion | flops 4294967296 | bytes 17825792 | tf_op jit(solution)/shard_map/krj,rm->kjm/dot_general | solution.py:42
  65.7 1.0 copy-done.4
  66.8 4.5 convolution_add_fusion
  71.2 1.1 copy.39
  72.6 1.1 cosine_multiply_fusion.1
  73.7 1.1 sine_multiply_fusion
  74.9 1.3 fusion.5
  76.2 1.5 add_bitcast_fusion
  77.8 3.8 copy.18
  81.6 0.6 dynamic-slice
  83.0 15.4 %sine_negate_fusion = f32[16,256,256]{2,1,0:T(8,128)} fusion(f32[256,256]{1,0:T(8,128)S(1)} %add_multiply_fusion, f32[16]{0:T(128)S(1)} %multiply_add_fusion.5), kind=kLoop, calls=%fused_computation.13 | loop fusion | flops 3145728 | bytes 4456512 | tf_op jit(solution)/shard_map/neg | solution.py:61
  98.4 51.2 %all-reduce.4.cloned.1.call-done = f32[2,256,2,256]{3,1,2,0:T(8,128)} async-done(((f32[2,256,2,256]{3,1,2,0:T(8,128)}), f32[2,256,2,256]{3,1,2,0:T(8,128)}) %all-reduce.4.cloned.1.call-update) | async-done | bytes 1048592 | tf_op jit(solution)/shard_map/psum | solution.py:106
  149.6 5.5 gather_fusion
  155.1 19.7 %subtract_multiply_fusion = f32[16,256,2,256]{3,1,2,0:T(8,128)S(1)} fusion(f32[16,256,2,256]{3,1,2,0:T(8,128)} %gather_fusion, f32[16,256,256]{2,1,0:T(8,128)} %sine_negate_fusion, pred[16]{0:T(512)(128)(4,1)S(1)} %compare_and_fusion, f32[16,256,512,1]{1,2,3,0:T(8,128)} %bitcast.73, f32[2,256,512,1]{2,1,0,3:T(8,128)S(1)} %bitcast.75), kind=kOutput, calls=%fused_computation.10 | convolution fusion | flops 6450839552 | bytes 30408720 | tf_op jit(solution)/shard_map/dot_general | solution.py:91
  174.8 6.5 %fusion.2 = f32[2,256,2,256]{3,0,2,1:T(2,128)S(1)} fusion(f32[16,256,2,256]{3,1,2,0:T(8,128)S(1)} %subtract_multiply_fusion, s32[16]{0:T(128)S(1)} %copy-done.5), kind=kOutput, calls=%fused_computation.8 | convolution fusion | flops 50331680 | bytes 9437248 | tf_op jit(solution)/shard_map/ps,pjcx->sjcx/dot_general | solution.py:115
  181.3 55.2 %all-reduce.5 = bf16[2,256,2,256]{3,0,2,1:T(2,128)(2,1)S(1)} all-reduce(f32[2,256,2,256]{3,0,2,1:T(2,128)S(1)} %fusion.2), channel_id=3, replica_groups=mesh['dp'=16,'group'=8] {'group'}, use_global_device_ids=true, to_apply=%region_1.2.clone | all-reduce | flops 262144 | bytes 1572864
  236.6 0.6 copy.21
  238.0 8.2 %broadcast_multiply_fusion = f32[32,32,16,256]{3,2,1,0:T(8,128)} fusion(f32[32,16,256]{2,1,0:T(8,128)S(1)} %select_add_fusion.2, f32[32,32,256]{2,1,0:T(8,128)S(1)} %select_add_fusion), kind=kLoop, calls=%fused_computation.12 | loop fusion | flops 4194304 | bytes 18350080 | tf_op jit(solution)/shard_map/mul | solution.py:33
  246.2 11.9 %fusion.1 = (bf16[32,512,256]{2,1,0:T(8,128)(2,1)}, bf16[32,512,256]{2,1,0:T(8,128)(2,1)}) fusion(f32[32,32,16,256]{3,2,1,0:T(8,128)} %broadcast_multiply_fusion), kind=kLoop, calls=%fused_computation.6 | loop fusion | flops 16777216 | bytes 33554432 | tf_op jit(solution)/shard_map/convert_element_type | solution.py:36
  258.1 305.9 %all-gather.3.cloned.1.call-done = bf16[256,32,2,256]{3,1,2,0:T(8,128)(2,1)} async-done(((bf16[2,32,2,256]{3,1,2,0:T(8,128)(2,1)}), bf16[256,32,2,256]{3,1,2,0:T(8,128)(2,1)}) %all-gather.3.cloned.1.call-update) | async-done | bytes 8388624 | tf_op jit(solution)/shard_map/all_gather | solution.py:120
  564.0 16.3 %copy.38 = bf16[16,8,2,32,2,256]{5,4,3,1,2,0:T(2,128)(2,1)} copy(bf16[16,8,2,32,2,256]{5,3,4,2,1,0:T(8,128)(2,1)} %bitcast.74) | data formatting | bytes 16777216 | tf_op jit(solution)/shard_map/reshape | solution.py:121
  580.3 14.1 %reshape_reshape.6 = bf16[32,256,512]{2,1,0:T(8,128)(2,1)} reshape(bf16[16,2,8,32,2,256]{5,4,3,2,1,0:T(2,128)(2,1)} %bitcast.72) | data formatting | bytes 16777216 | tf_op jit(solution)/shard_map/reshape;reshape | solution.py:51
  594.4 9.6 %convolution_bitcast_fusion = f32[512,512]{1,0:T(8,128)S(1)} fusion(bf16[32,512,256]{2,1,0:T(8,128)(2,1)} %get-tuple-element.5, bf16[32,256,512]{2,1,0:T(8,128)(2,1)} %reshape_reshape.6), kind=kOutput, calls=%fused_computation.17 | convolution fusion | flops 4294967296 | bytes 17825792 | tf_op jit(solution)/shard_map/krj,kjm->rm/dot_general | solution.py:53
  604.0 8.1 %fusion.7 = f32[512,512]{1,0:T(8,128)} fusion(f32[512,512]{1,0:T(8,128)S(1)} %convolution_bitcast_fusion, bf16[32,512,256]{2,1,0:T(8,128)(2,1)} %get-tuple-element.6, bf16[32,256,512]{2,1,0:T(8,128)(2,1)S(1)} %copy-done.3), kind=kOutput, calls=%fused_computation.19 | convolution fusion | flops 4295229440 | bytes 18874368 | tf_op jit(solution)/shard_map/krj,kjm->rm/dot_general | solution.py:52
  612.1 1.9 reshape_reshape.7
  614.0 2.8 multiply_add_fusion
  (41 shorter events, 1.8 us)
Async XLA Ops:
  6.5 68.3 %copy-start = (bf16[16,256,256]{2,1,0:T(8,128)(2,1)S(1)}, bf16[16,256,256]{2,1,0:T(8,128)(2,1)}, u32[]{:S(2)}) copy-start(bf16[16,256,256]{2,1,0:T(8,128)(2,1)} %param.6) | copy-start | bytes 6291460
  6.5 143.0 %all-reduce.4.cloned.1.call-start = ((), (), s32[]{:S(2)}) async-start(), calls=%async_computation | async-start | bytes 2097152 | tf_op jit(solution)/shard_map/psum | solution.py:106
  56.1 9.6 %copy-start.2 = (bf16[8192,512,1]{1,0,2:T(8,128)(2,1)S(1)}, bf16[8192,512,1]{1,0,2:T(8,128)(2,1)}, u32[]{:S(2)}) copy-start(bf16[8192,512,1]{1,0,2:T(8,128)(2,1)} %reshape.603) | copy-start | bytes 25165828
  56.1 10.6 %copy-start.4 = (bf16[2,8192,256]{1,2,0:T(8,128)(2,1)S(1)}, bf16[2,8192,256]{1,2,0:T(8,128)(2,1)}, u32[]{:S(2)}) copy-start(bf16[2,8192,256]{1,2,0:T(8,128)(2,1)} %convert_element_type.186) | copy-start | bytes 25165828
  66.8 8.1 %copy-start.5 = (s32[16]{0:T(128)S(1)}, s32[16]{0:T(128)}, u32[]{:S(2)}) copy-start(s32[16]{0:T(128)} %param.8) | copy-start | bytes 196
  72.3 491.7 %all-gather.3.cloned.1.call-start = ((), (), s32[]{:S(2)}) async-start(), calls=%async_computation.1 | async-start | bytes 8454144 | tf_op jit(solution)/shard_map/all_gather | solution.py:120
  77.8 3.8 copy-start.8
  77.8 5.1 copy-start.7
  174.8 62.4 %copy-start.6 = (s32[32]{0:T(128)S(1)}, s32[32]{0:T(128)}, u32[]{:S(2)}) copy-start(s32[32]{0:T(128)} %param.7) | copy-start | bytes 388
  594.4 9.6 %copy-start.3 = (bf16[32,256,512]{2,1,0:T(8,128)(2,1)S(1)}, bf16[32,256,512]{2,1,0:T(8,128)(2,1)}, u32[]{:S(2)}) copy-start(bf16[32,256,512]{2,1,0:T(8,128)(2,1)} %reshape_reshape.6) | copy-start | bytes 25165828
  604.0 12.8 %copy-start.1 = (bf16[16,256,256]{2,1,0:T(8,128)(2,1)S(1)}, bf16[16,256,256]{2,1,0:T(8,128)(2,1)}, u32[]{:S(2)}) copy-start(bf16[16,256,256]{2,1,0:T(8,128)(2,1)} %param.6) | copy-start | bytes 6291460
Sparse Core Ops, SparseCore 0:
  72.5 77.0 all-reduce.3
  237.4 326.6 all-gather.2

commit v3 on v1

--- a/solution.py
+++ b/solution.py
@@ -112,7 +112,7 @@
     onehot = (batch_slot[:, None] == jnp.arange(ORI_DEV, dtype=jnp.int32)[None, :]).astype(
         jnp.float32
     )
-    local_grads = jnp.einsum("ps,pjcx->sjcx", onehot, weighted, precision=lax.Precision.HIGHEST)
+    local_grads = jnp.sum(onehot[:, :, None, None, None] * weighted[:, None], axis=0)
     slice_grads = lax.psum(local_grads, "group").astype(jnp.bfloat16)
     all_grads = lax.all_gather(slice_grads, "dp", axis=0, tiled=True)
     strip = backproject(all_grads, orientation, slab_start, slab_len, strip_start, strip_len)

time: 371 us -> 357 us (0.962)
  matrix products: 61.3 us -> 50.8 us
  local copies, waits for them, and re-layouts: 67.2 us -> 62 us
    all_gather x1 -> x0, local copies, waits for them, and re-layouts: 12 us -> none  [per_device(): all_grads = lax.all_gather(slice_grads, 'dp', axis=0, tiled=True)]
    reshape x0 -> x1, local copies, waits for them, and re-layouts: none -> 7.53 us  [backproject(): flat = slice_grads.reshape(count, length, 2 * length)]
    dot_general x1 -> x0, matrix products: 6.47 us -> none  [per_device(): jnp.einsum('ps,pjcx->sjcx', onehot, weighted, precision=lax.Precision.HIG...]
  transfers between devices with their start and end apart: 2 -> 2, of which waited for: 2 -> 2; matrix products, arithmetic and copies ran while one was open for 12% -> 13% of each run, Pallas kernels for 0% -> 0%
where the time goes in v3:
time: 357 us; the launch traced here: 356 us
  waiting for transfers between devices  122 us (34%)
  local copies, waits for them, and re-layouts  62 us (17%)
  blocking collectives  55.9 us (16%)
  other arithmetic  51.6 us (14%)
  matrix products  50.8 us (14%)
  between operations  13.7 us (4%)
    all_gather x1, waiting for transfers between devices, per_device(): all_grads = lax.all_gather(slice_grads, 'dp', axis=0, tiled=True)  69.1 us
    psum x1, blocking collectives, per_device(): slice_grads = lax.psum(local_grads, 'group').astype(jnp.bfloat16)  55.9 us
    psum x1, waiting for transfers between devices, per_device(): slices = lax.psum(partial_value, 'group')  52.4 us
    dot_general x1, matrix products, spectra(): jnp.dot(flat, complex_mat, precision=lax.Precision.HIGH, preferred_elemen...  18.9 us
    convert_element_type x2, other arithmetic, slice_matrix(): low = (full - high.astype(jnp.float32)).astype(jnp.bfloat16)  18.6 us
    neg x1, other arithmetic, contrast(): return -jnp.sin(defocus[:, None, None] * radius[None] + 0.1)  15.4 us
    reshape x1, local copies, waits for them, and re-layouts, per_device(): planes = volume.reshape(slab_len * length, 2 * length)  14.1 us
    convert_element_type x1, local copies, waits for them, and re-layouts, slice_matrix(): low = (full - high.astype(jnp.float32)).astype(jnp.bfloat16)  13.5 us
  transfers between devices with their start and end apart: 2, of which 2 were waited for; matrix products, arithmetic and copies ran while one was open for 13% of the time, Pallas kernels for 0%

profile of v3, /device:TPU:1, one launch (start us, length us, event | category | flops | bytes accessed | tf_op | source)
XLA Modules:
  0.0 355.6 jit_solution(9605076136704682321)
XLA Ops:
  6.5 0.9 fusion.32
  7.6 0.3 select_add_fusion.1
  8.0 0.3 select_add_fusion.3
  8.3 6.7 %fusion = (bf16[2,32,256,256]{2,1,3,0:T(8,128)(2,1)}, bf16[2,32,256,256]{2,1,3,0:T(8,128)(2,1)}) fusion(f32[2,256,256]{1,2,0:T(8,128)S(1)} %select_add_fusion.1, f32[2,32,256]{1,2,0:T(8,128)S(1)} %select_add_fusion.3), kind=kLoop, calls=%fused_computation.3 | loop fusion | flops 20971520 | bytes 17367040 | tf_op jit(solution)/shard_map/convert_element_type | solution.py:36
  15.0 13.5 %convert_element_type.190 = bf16[2,8192,256]{1,2,0:T(8,128)(2,1)} reshape(bf16[2,32,256,256]{2,1,3,0:T(8,128)(2,1)} %get-tuple-element.8) | data formatting | bytes 16777216 | tf_op jit(solution)/shard_map/convert_element_type | solution.py:35
  28.5 14.1 %reshape.623 = bf16[8192,512,1]{1,0,2:T(8,128)(2,1)} reshape(bf16[32,256,2,256]{3,2,1,0:T(2,128)(2,1)} %param.5) | data formatting | bytes 16777216 | tf_op jit(solution)/shard_map/reshape | solution.py:104
  42.6 13.5 %convert_element_type.193 = bf16[2,8192,256]{1,2,0:T(8,128)(2,1)} reshape(bf16[2,32,256,256]{2,1,3,0:T(8,128)(2,1)} %get-tuple-element.7) | data formatting | bytes 16777216 | tf_op jit(solution)/shard_map/convert_element_type | solution.py:36
  56.1 9.6 %fusion.33 = f32[2,256,512]{2,1,0:T(8,128)S(1)} fusion(bf16[2,8192,256]{1,2,0:T(8,128)(2,1)} %convert_element_type.190, bf16[8192,512,1]{1,0,2:T(8,128)(2,1)} %reshape.623), kind=kOutput, calls=%fused_computation.96 | convolution fusion | flops 4294967296 | bytes 17825792 | tf_op jit(solution)/shard_map/krj,rm->kjm/dot_general | solution.py:42
  65.7 1.0 copy-done.4
  66.8 4.5 %convolution_add_fusion = f32[2,256,512]{2,1,0:T(8,128)S(1)} fusion(f32[2,256,512]{2,1,0:T(8,128)S(1)} %fusion.33, bf16[2,8192,256]{1,2,0:T(8,128)(2,1)S(1)} %copy-done.4, bf16[8192,512,1]{1,0,2:T(8,128)(2,1)S(1)} %copy-done.2), kind=kOutput, calls=%fused_computation.18 | convolution fusion | flops 4295229440 | bytes 18874368 | tf_op jit(solution)/shard_map/krj,rm->kjm/dot_general | solution.py:43
  71.2 1.1 copy.40
  72.3 0.2 all-gather.2.cloned.1.call-start
  72.6 1.1 cosine_multiply_fusion.1
  73.7 1.1 sine_multiply_fusion
  74.9 1.3 fusion.3
  76.2 1.5 add_bitcast_fusion
  77.8 3.8 %copy.25 = f32[16,256,2,256]{1,3,2,0:T(8,128)} copy(f32[16,256,2,256]{1,3,0,2:T(8,128)S(1)} %add_bitcast_fusion) | data formatting | bytes 16777216 | tf_op jit(solution)/shard_map/add | solution.py:78
  81.8 15.4 %sine_negate_fusion = f32[16,256,256]{2,1,0:T(8,128)} fusion(f32[256,256]{1,0:T(8,128)S(1)} %add_multiply_fusion, f32[16]{0:T(128)S(1)} %multiply_add_fusion.5), kind=kLoop, calls=%fused_computation.11 | loop fusion | flops 3145728 | bytes 4456512 | tf_op jit(solution)/shard_map/neg | solution.py:61
  97.2 52.4 %all-reduce.3.cloned.1.call-done = f32[2,256,2,256]{3,1,2,0:T(8,128)} async-done(((f32[2,256,2,256]{3,1,2,0:T(8,128)}), f32[2,256,2,256]{3,1,2,0:T(8,128)}) %all-reduce.3.cloned.1.call-update) | async-done | bytes 1048592 | tf_op jit(solution)/shard_map/psum | solution.py:106
  149.7 5.5 %gather_fusion = f32[16,256,2,256]{3,1,2,0:T(8,128)} fusion(f32[2,256,2,256]{3,1,2,0:T(8,128)} %all-reduce.3.cloned.1.call-done, s32[1024]{0:T(1024)S(1)} %pad_clamp_fusion), kind=kCustom, calls=%fused_computation | custom fusion | bytes 16777280 | tf_op jit(solution)/shard_map/jit(_take)/gather | solution.py:109
  155.2 18.9 %subtract_multiply_fusion = f32[16,256,2,256]{3,1,2,0:T(8,128)S(1)} fusion(f32[16,256,2,256]{3,1,2,0:T(8,128)} %gather_fusion, f32[16,256,256]{2,1,0:T(8,128)} %sine_negate_fusion, pred[16]{0:T(512)(128)(4,1)S(1)} %compare_and_fusion, f32[16,256,512,1]{1,2,3,0:T(8,128)} %bitcast.64, f32[2,256,512,1]{2,1,0,3:T(8,128)S(1)} %bitcast.70), kind=kOutput, calls=%fused_computation.8 | convolution fusion | flops 6450839552 | bytes 30408720 | tf_op jit(solution)/shard_map/dot_general | solution.py:91
  174.2 1.5 multiply_reduce_fusion
  175.7 55.9 %all-reduce.4 = bf16[2,256,2,256]{3,1,2,0:T(8,128)(2,1)} all-reduce(f32[2,256,2,256]{3,1,2,0:T(8,128)S(1)} %multiply_reduce_fusion), channel_id=1, replica_groups=mesh['dp'=16,'group'=8] {'group'}, use_global_device_ids=true, to_apply=%region_2.3 | all-reduce | flops 262144 | bytes 1572864 | tf_op jit(solution)/shard_map/psum | solution.py:116
  232.0 0.3 select_add_fusion
  232.3 8.2 %broadcast_multiply_fusion = f32[32,32,16,256]{3,2,1,0:T(8,128)} fusion(f32[32,16,256]{2,1,0:T(8,128)S(1)} %select_add_fusion.2, f32[32,32,256]{2,1,0:T(8,128)S(1)} %select_add_fusion), kind=kLoop, calls=%fused_computation.10 | loop fusion | flops 4194304 | bytes 18350080 | tf_op jit(solution)/shard_map/mul | solution.py:33
  240.6 11.9 %fusion.1 = (bf16[32,512,256]{2,1,0:T(8,128)(2,1)}, bf16[32,512,256]{2,1,0:T(8,128)(2,1)}) fusion(f32[32,32,16,256]{3,2,1,0:T(8,128)} %broadcast_multiply_fusion), kind=kLoop, calls=%fused_computation.6 | loop fusion | flops 16777216 | bytes 33554432 | tf_op jit(solution)/shard_map/convert_element_type | solution.py:36
  252.5 69.1 %all-gather.2.cloned.1.call-done = bf16[32,256,2,256]{3,1,2,0:T(8,128)(2,1)} async-done(((bf16[2,256,2,256]{3,1,2,0:T(8,128)(2,1)}), bf16[32,256,2,256]{3,1,2,0:T(8,128)(2,1)}) %all-gather.2.cloned.1.call-update) | async-done | bytes 8388624 | tf_op jit(solution)/shard_map/all_gather | solution.py:117
  321.5 7.5 %copy.38 = bf16[32,2,32,8,256]{4,3,1,2,0:T(8,128)(2,1)} copy(bf16[32,2,32,8,256]{4,3,2,1,0:T(8,128)(2,1)} %bitcast.65) | data formatting | bytes 16777216 | tf_op jit(solution)/shard_map/reshape | solution.py:51
  329.1 9.6 %convolution_bitcast_fusion = f32[512,512]{1,0:T(8,128)S(1)} fusion(bf16[32,512,256]{2,1,0:T(8,128)(2,1)} %get-tuple-element.5, bf16[32,256,512]{2,1,0:T(8,128)(2,1)} %bitcast.66), kind=kOutput, calls=%fused_computation.15 | convolution fusion | flops 4294967296 | bytes 17825792 | tf_op jit(solution)/shard_map/krj,kjm->rm/dot_general | solution.py:53
  338.7 5.5 %fusion.5 = f32[512,512]{1,0:T(8,128)} fusion(f32[512,512]{1,0:T(8,128)S(1)} %convolution_bitcast_fusion, bf16[32,512,256]{2,1,0:T(8,128)(2,1)S(1)} %bitcast.69, bf16[32,256,512]{2,1,0:T(8,128)(2,1)S(1)} %bitcast.67), kind=kOutput, calls=%fused_computation.17 | convolution fusion | flops 4295229440 | bytes 18874368 | tf_op jit(solution)/shard_map/krj,kjm->rm/dot_general | solution.py:52
  344.1 1.9 reshape_reshape.3
  346.0 2.8 multiply_add_fusion
  (41 shorter events, 0.9 us)
Async XLA Ops:
  6.5 68.4 %copy-start = (bf16[16,256,256]{2,1,0:T(8,128)(2,1)S(1)}, bf16[16,256,256]{2,1,0:T(8,128)(2,1)}, u32[]{:S(2)}) copy-start(bf16[16,256,256]{2,1,0:T(8,128)(2,1)} %param.6) | copy-start | bytes 6291460
  6.5 143.1 %all-reduce.3.cloned.1.call-start = ((), (), s32[]{:S(2)}) async-start(), calls=%async_computation | async-start | bytes 2097152 | tf_op jit(solution)/shard_map/psum | solution.py:106
  56.1 9.6 %copy-start.2 = (bf16[8192,512,1]{1,0,2:T(8,128)(2,1)S(1)}, bf16[8192,512,1]{1,0,2:T(8,128)(2,1)}, u32[]{:S(2)}) copy-start(bf16[8192,512,1]{1,0,2:T(8,128)(2,1)} %reshape.623) | copy-start | bytes 25165828
  56.1 10.6 %copy-start.4 = (bf16[2,8192,256]{1,2,0:T(8,128)(2,1)S(1)}, bf16[2,8192,256]{1,2,0:T(8,128)(2,1)}, u32[]{:S(2)}) copy-start(bf16[2,8192,256]{1,2,0:T(8,128)(2,1)} %convert_element_type.193) | copy-start | bytes 25165828
  66.8 8.1 %copy-start.5 = (s32[16]{0:T(128)S(1)}, s32[16]{0:T(128)}, u32[]{:S(2)}) copy-start(s32[16]{0:T(128)} %param.8) | copy-start | bytes 196
  72.3 249.2 %all-gather.2.cloned.1.call-start = ((), (), s32[]{:S(2)}) async-start(), calls=%async_computation.1 | async-start | bytes 8912896 | tf_op jit(solution)/shard_map/all_gather | solution.py:117
  77.8 3.8 %copy-start.7 = (s32[16]{0:T(128)S(1)}, s32[16]{0:T(128)}, u32[]{:S(2)}) copy-start(s32[16]{0:T(128)} %param.9) | copy-start | bytes 196
  174.1 57.5 %copy-start.6 = (s32[32]{0:T(128)S(1)}, s32[32]{0:T(128)}, u32[]{:S(2)}) copy-start(s32[32]{0:T(128)} %param.7) | copy-start | bytes 388
  321.5 17.1 %slice-start = ((s8[8388608]{0:T(1024)(128)(4,1)}), s8[4194304]{0:T(1024)(128)(4,1)S(1)}, s32[]{:S(2)}) async-start(s8[8388608]{0:T(1024)(128)(4,1)} %bitcast.68), calls=%async_computation.2 | async-start | bytes 8388608
  329.1 9.6 %copy-start.3 = (bf16[32,2,32,8,256]{4,3,1,2,0:T(8,128)(2,1)S(1)}, bf16[32,2,32,8,256]{4,3,1,2,0:T(8,128)(2,1)}, u32[]{:S(2)}) copy-start(bf16[32,2,32,8,256]{4,3,1,2,0:T(8,128)(2,1)} %copy.38) | copy-start | bytes 25165828
  329.1 9.6 %slice-start.1 = ((s8[8388608]{0:T(1024)(128)(4,1)}), s8[4194304]{0:T(1024)(128)(4,1)S(1)}, s32[]{:S(2)}) async-start(s8[8388608]{0:T(1024)(128)(4,1)} %bitcast.68), calls=%async_computation.3 | async-start | bytes 8388608
  338.7 10.1 %copy-start.1 = (bf16[16,256,256]{2,1,0:T(8,128)(2,1)S(1)}, bf16[16,256,256]{2,1,0:T(8,128)(2,1)}, u32[]{:S(2)}) copy-start(bf16[16,256,256]{2,1,0:T(8,128)(2,1)} %param.6) | copy-start | bytes 6291460
Sparse Core Ops, SparseCore 0:
  72.5 77.1 all-reduce.2
  231.7 89.7 all-gather.1
